TPU v7x, 32 devices: a whole 2x2x4 slice. The times are simulated.
32 devices in a mesh: vocab: 8 (over z, x), batch: 4 (over y, core).
Axes of the slice: x: 2, y: 2, z: 4, core: 2. Of those that a mesh axis runs over, the one named last changes fastest.
Arguments:
- hidden: bfloat16 [256, 1024], P(('vocab', 'batch'))
- embedding: bfloat16 [8192, 1024], P('vocab')
- block_counts: int32 [64], P('vocab'), may hold values from 1 to 4095
- lang_blocks: int32 [200, 64], replicated, may hold values from -1 to 63, as said below
- sent_lang: int32 [4], replicated, may hold values from 0 to 199
- targets: int32 [256], replicated, may hold values from 0 to 8191, as said below
Outputs:
- token_loss: float32 [256], P(('vocab', 'batch'))
- grad_embed: bfloat16 [8192, 1024], P(('vocab', 'batch'))
Inputs may be any that keep to these rules, and one draw needn't show every extreme that they name: `lang_blocks`: each list holds distinct block numbers and then -1 padding; the first entry of every list is block 0; at least 16 entries are blocks, and some language fills all 64 entries. `targets`: the target of token t lies in a block listed for the language of sentence t // 64.
All inputs are finite; a program needn't handle non-finite values.
Results may differ from a plain program's by a relative error of at most 0.0075.
Values may be sent and summed in bfloat16 or wider, within the bound.
No kernel may reach another device: no remote copies, remote signals or barrier semaphores. Data moves between devices by JAX's collectives and lax.ppermute only.
A program may use at most 64 MiB of HBM per device.

v0:
```python
import jax
import jax.numpy as jnp
from jax import lax
from jax.sharding import PartitionSpec as P

SEQ = 64


masked_fill = -1e30


def body(hidden, embedding, block_counts, lang_blocks, sent_lang, targets):
    tok_dev = hidden.shape[0]
    vocab_count = lax.axis_size("vocab")
    batch_count = lax.axis_size("batch")
    vocab_index = lax.axis_index("vocab")
    batch_index = lax.axis_index("batch")
    local_rows = embedding.shape[0]
    local_blocks = block_counts.shape[0]
    block_width = local_rows // local_blocks
    gathered = lax.all_gather(hidden, "vocab", axis=0, tiled=True)
    token_count = gathered.shape[0]
    token_ids = (
        (jnp.arange(vocab_count, dtype=jnp.int32)[:, None] * batch_count + batch_index) * tok_dev
        + jnp.arange(tok_dev, dtype=jnp.int32)[None, :]
    ).reshape(-1)
    target_ids = lax.dynamic_index_in_dim(
        targets.reshape(vocab_count, batch_count, tok_dev), batch_index, 1, keepdims=False
    ).reshape(-1)
    sentence = token_ids // SEQ
    sentence_hit = sentence[:, None] == jnp.arange(sent_lang.shape[0], dtype=jnp.int32)[None, :]
    token_language = jnp.sum(jnp.where(sentence_hit, sent_lang[None, :], 0), axis=1)
    block_ids = vocab_index * local_blocks + jnp.arange(local_blocks, dtype=jnp.int32)
    member = jnp.any(lang_blocks[:, :, None] == block_ids[None, None, :], axis=1).astype(
        jnp.float32
    )
    language_hit = (
        token_language[:, None] == jnp.arange(lang_blocks.shape[0], dtype=jnp.int32)[None, :]
    ).astype(jnp.float32)
    allowed = jnp.dot(language_hit, member, precision=lax.Precision.HIGHEST) > 0.5
    allowed_cells = allowed[:, :, None]
    raw_scores = lax.dot_general(
        gathered, embedding, (((1,), (1,)), ((), ())), preferred_element_type=jnp.float32
    )
    log_sampling = jnp.log(block_counts.astype(jnp.float32))
    logits = (
        raw_scores.reshape(token_count, local_blocks, block_width) - log_sampling[None, :, None]
    )
    masked = jnp.where(allowed_cells, logits, masked_fill)
    word_ids = (vocab_index * local_rows + jnp.arange(local_rows, dtype=jnp.int32)).reshape(
        local_blocks, block_width
    )
    is_target = word_ids[None, :, :] == target_ids[:, None, None]
    local_peak = jnp.max(masked, axis=(1, 2))
    local_target = jnp.sum(jnp.where(is_target, logits, 0.0), axis=(1, 2))
    peak_value = lax.pmax(local_peak, "vocab")
    local_total = jnp.sum(
        jnp.where(allowed_cells, jnp.exp(masked - peak_value[:, None, None]), 0.0), axis=(1, 2)
    )
    denominator, target_logit = lax.psum((local_total, local_target), "vocab")
    log_total = peak_value + jnp.log(denominator)
    every_loss = log_total - target_logit
    token_loss = lax.dynamic_slice_in_dim(every_loss, vocab_index * tok_dev, tok_dev, 0)
    softmax_weights = jnp.where(allowed_cells, jnp.exp(logits - log_total[:, None, None]), 0.0)
    grad_logits = (
        (softmax_weights - is_target.astype(jnp.float32))
        .astype(jnp.bfloat16)
        .reshape(token_count, local_rows)
    )
    columns = lax.all_to_all(grad_logits, "batch", split_axis=1, concat_axis=0, tiled=True)
    everyone = lax.all_gather(gathered, "batch", axis=0, tiled=True)
    summed = jnp.zeros((columns.shape[1], gathered.shape[1]), jnp.float32)
    for source in range(batch_count):
        slice_grad = columns[source * token_count : (source + 1) * token_count]
        slice_rows = everyone[source * token_count : (source + 1) * token_count]
        contribution = lax.dot_general(
            slice_grad, slice_rows, (((0,), (0,)), ((), ())), preferred_element_type=jnp.float32
        )
        rounded = lax.optimization_barrier(contribution.astype(jnp.bfloat16))
        summed = summed + rounded.astype(jnp.float32)
    grad_embed = summed.astype(jnp.bfloat16)
    return (token_loss, grad_embed)


def solution(mesh):
    in_specs = (P(("vocab", "batch"), None), P("vocab", None), P("vocab"), P(), P(), P())
    out_specs = (P(("vocab", "batch")), P(("vocab", "batch"), None))
    return jax.shard_map(body, mesh=mesh, in_specs=in_specs, out_specs=out_specs, check_vma=False)
```

profile of v0, /device:TPU:0, one launch (start us, length us, event | category | flops | bytes accessed | tf_op | source)
XLA Modules:
  0.0 92.3 jit_solution(3741572874803002125)
XLA Ops:
  0.7 0.8 convert_log_fusion
  1.6 0.1 add.93
  1.7 1.0 %compare_reduce_fusion = pred[200,8]{0,1:T(8,128)(4,1)S(1)} fusion(s32[200,64]{0,1:T(8,128)} %param.9, s32[8]{0:T(128)S(1)} %iota_add_fusion.1), kind=kLoop, calls=%fused_computation.7 | loop fusion | flops 203200 | bytes 52832 | tf_op jit(solution)/shard_map/reduce_or | solution.py:34
  2.7 0.7 select_reduce_fusion.1
  3.5 0.2 convolution_compare_fusion
  3.7 0.1 copy.13
  3.8 0.8 reshape.91
  4.6 0.1 eq.66
  4.7 32.5 %all_gather.6 = bf16[64,1024]{1,0:T(8,128)(2,1)S(1)} all-gather(bf16[8,1024]{1,0:T(8,128)(2,1)} %param.6), channel_id=1, replica_groups=mesh['vocab'=8,'batch'=4] {'vocab'}, dimensions={0}, use_global_device_ids=true | all-gather | bytes 147456 | tf_op jit(solution)/shard_map/all_gather | solution.py:21
  37.2 0.1 broadcast_in_dim.53
  37.3 0.9 fusion.3
  38.2 21.3 %pmax.7 = f32[64]{0:T(128)S(1)} all-reduce(f32[64]{0:T(128)S(1)} %get-tuple-element.8), channel_id=1, replica_groups=mesh['vocab'=8,'batch'=4] {'vocab'}, use_global_device_ids=true, to_apply=%region_3.4 | all-reduce | flops 64 | bytes 512 | tf_op jit(solution)/shard_map/pmax | solution.py:56
  59.5 0.3 fusion
  59.8 17.1 %all-reduce = (f32[64]{0:T(128)S(1)}, f32[64]{0:T(128)S(1)}) all-reduce(f32[64]{0:T(128)S(1)} %get-tuple-element.3, f32[64]{0:T(128)S(1)} %get-tuple-element.2), channel_id=1, replica_groups=mesh['vocab'=8,'batch'=4] {'vocab'}, use_global_device_ids=true, to_apply=%region_5.6 | all-reduce | flops 128 | bytes 1024 | tf_op jit(solution)/shard_map/psum | solution.py:60
  76.9 0.1 fusion.2
  77.1 0.7 copy.21
  77.7 3.3 %all-to-all-start = ((bf16[64,4,256]{2,0,1:T(8,128)(2,1)}), bf16[64,4,256]{2,0,1:T(8,128)(2,1)S(1)}, u32[]{:S(2)}, u32[]{:S(2)}) async-start(bf16[64,4,256]{2,0,1:T(8,128)(2,1)} %bitcast.32), calls=%async_computation | async-start | bytes 262144 | tf_op jit(solution)/shard_map/all_to_all | solution.py:70
  81.1 8.2 %all_gather.7 = bf16[256,1024]{1,0:T(8,128)(2,1)S(1)} all-gather(bf16[64,1024]{1,0:T(8,128)(2,1)S(1)} %all_gather.6), channel_id=1, replica_groups=mesh['vocab'=8,'batch'=4] {'batch'}, dimensions={0}, use_global_device_ids=true | all-gather | bytes 655360 | tf_op jit(solution)/shard_map/all_gather | solution.py:71
  89.3 0.6 dynamic_slice.8
  89.9 0.3 convolution_convert_fusion
  90.2 0.3 convolution_convert_fusion.1
  90.5 0.3 convolution_convert_fusion.2
  90.9 0.3 convolution_convert_fusion.3
  91.2 1.1 %add_convert_fusion = bf16[256,1024]{1,0:T(8,128)(2,1)} fusion(bf16[256,1024]{1,0:T(8,128)(2,1)S(1)} %convolution_convert_fusion, bf16[256,1024]{1,0:T(8,128)(2,1)S(1)} %convolution_convert_fusion.1, bf16[256,1024]{1,0:T(8,128)(2,1)S(1)} %convolution_convert_fusion.2, bf16[256,1024]{1,0:T(8,128)(2,1)S(1)} %convolution_convert_fusion.3), kind=kLoop, calls=%fused_computation.6 | loop fusion | flops 2097152 | bytes 2621440 | tf_op jit(solution)/shard_map/convert_element_type | solution.py:81
  (11 shorter events, 0.2 us)
Async XLA Ops:
  0.6 36.7 %copy-start = (bf16[1024,1024]{1,0:T(8,128)(2,1)S(1)}, bf16[1024,1024]{1,0:T(8,128)(2,1)}, u32[]{:S(2)}) copy-start(bf16[1024,1024]{1,0:T(8,128)(2,1)} %param.7) | copy-start | bytes 6291460
  77.7 12.2 %all-to-all-start = ((bf16[64,4,256]{2,0,1:T(8,128)(2,1)}), bf16[64,4,256]{2,0,1:T(8,128)(2,1)S(1)}, u32[]{:S(2)}, u32[]{:S(2)}) async-start(bf16[64,4,256]{2,0,1:T(8,128)(2,1)} %bitcast.32), calls=%async_computation | async-start | bytes 262144 | tf_op jit(solution)/shard_map/all_to_all | solution.py:70
where the time goes:
time: 92.7 us; the launch traced here: 92.3 us
  blocking collectives  79.2 us (85%)
  other arithmetic  4.2 us (5%)
  starting transfers between devices  3.33 us (4%)
  local copies, waits for them, and re-layouts  2.52 us (3%)
  matrix products  2.32 us (3%)
    all_gather x1, blocking collectives, body(): gathered = lax.all_gather(hidden, 'vocab', axis=0, tiled=True)  32.5 us
    pmax x1, blocking collectives, body(): peak_value = lax.pmax(local_peak, 'vocab')  21.3 us
    psum x1, blocking collectives, body(): denominator, target_logit = lax.psum((local_total, local_target), 'vocab')  17.1 us
    all_gather x1, blocking collectives, body(): everyone = lax.all_gather(gathered, 'batch', axis=0, tiled=True)  8.24 us
    all_to_all x1, starting transfers between devices, body(): lax.all_to_all(grad_logits, 'batch', split_axis=1, concat_axis=0, tiled=T...  3.33 us
  transfers between devices with their start and end apart: 1, of which 0 were waited for; matrix products, arithmetic and copies ran while one was open for 1% of the time, Pallas kernels for 0%

commit v1 on v0

v1 whole, which is shorter than its diff:
```python
import jax
import jax.numpy as jnp
from jax import lax
from jax.sharding import PartitionSpec as P

SEQ = 64


masked_fill = float(jnp.finfo(jnp.float32).min)


def centre_first(count):
    return sorted(range(count), key=lambda i: (abs(i // 2 - count // 4), i // 2, -i))


def body(hidden, embedding, block_counts, lang_blocks, sent_lang, targets):
    tok_dev, width = hidden.shape
    vocab_count = lax.axis_size("vocab")
    batch_count = lax.axis_size("batch")
    vocab_index = lax.axis_index("vocab")
    batch_index = lax.axis_index("batch")
    local_rows = embedding.shape[0]
    local_blocks = block_counts.shape[0]
    block_width = local_rows // local_blocks
    own_rows = local_rows // batch_count
    own_blocks = own_rows // block_width
    group_tokens = vocab_count * tok_dev
    order = centre_first(vocab_count)
    both = ("vocab", "batch")
    groups = [[v * batch_count + b for v in order] for b in range(batch_count)]

    copies = jnp.broadcast_to(hidden[None], (vocab_count, tok_dev, width))
    gathered = lax.all_to_all(copies, both, 0, 0, tiled=True, axis_index_groups=groups)
    gathered = gathered.reshape(group_tokens, width)
    pieces = [gathered]
    for step in range(1, batch_count):
        pairs = [(b, b ^ step) for b in range(batch_count)]
        pieces.append(lax.ppermute(gathered, "batch", pairs))
    everyone = jnp.concatenate(pieces, axis=0)

    sources = batch_index ^ jnp.arange(batch_count, dtype=jnp.int32)
    places = jnp.array(order, jnp.int32)
    token_ids = (
        (places[None, :, None] * batch_count + sources[:, None, None]) * tok_dev
        + jnp.arange(tok_dev, dtype=jnp.int32)[None, None, :]
    ).reshape(batch_count, group_tokens)
    target_table = targets.reshape(vocab_count, batch_count, tok_dev)
    target_table = jnp.stack([target_table[v] for v in order], axis=1)
    target_ids = jnp.stack(
        [
            lax.dynamic_index_in_dim(target_table, batch_index ^ step, 0, keepdims=False)
            for step in range(batch_count)
        ]
    ).reshape(batch_count, group_tokens)

    block_ids = vocab_index * local_blocks + jnp.arange(local_blocks, dtype=jnp.int32)
    sentence_lists = lang_blocks[sent_lang]
    member = jnp.any(sentence_lists[:, None, :] == block_ids[None, :, None], axis=2)
    sentence_ids = jnp.arange(sent_lang.shape[0], dtype=jnp.int32)
    sentence_hit = (token_ids // SEQ)[None] == sentence_ids[:, None, None]
    allowed = jnp.any(member[:, :, None, None] & sentence_hit[:, None], axis=0)
    log_sampling = jnp.log(block_counts.astype(jnp.float32))

    own_allowed = allowed[:, 0][:, None, :]
    logits = lax.dot_general(
        embedding, gathered, (((1,), (1,)), ((), ())), preferred_element_type=jnp.float32
    ).reshape(local_blocks, block_width, group_tokens) - log_sampling[:, None, None]
    word_ids = (vocab_index * local_rows + jnp.arange(local_rows, dtype=jnp.int32)).reshape(
        local_blocks, block_width
    )
    is_target = word_ids[:, :, None] == target_ids[0][None, None, :]
    local_peak = jnp.max(jnp.where(own_allowed, logits, masked_fill), axis=(0, 1))
    local_total = jnp.sum(
        jnp.where(own_allowed, jnp.exp(logits - local_peak[None, None, :]), 0.0), axis=(0, 1)
    )
    local_target = jnp.sum(jnp.where(is_target, logits, 0.0), axis=(0, 1))
    blank = jnp.zeros_like(local_peak)
    stats = jnp.stack([local_peak, local_total, local_target] + [blank] * 5)
    stats = jnp.broadcast_to(stats[None], (vocab_count * batch_count,) + stats.shape)
    stats = lax.all_to_all(stats, both, 0, 0, tiled=True)
    stats = stats.reshape(vocab_count, batch_count, 8, group_tokens)
    peak = jnp.max(stats[:, :, 0], axis=0)
    total = jnp.sum(stats[:, :, 1] * jnp.exp(stats[:, :, 0] - peak[None]), axis=0)
    log_total = peak + jnp.log(total)
    target_logit = jnp.sum(stats[:, :, 2], axis=0)
    every_loss = lax.dynamic_index_in_dim(log_total - target_logit, batch_index, 0, keepdims=False)
    my_place = jnp.sum(jnp.where(places == vocab_index, jnp.arange(vocab_count), 0))
    token_loss = lax.dynamic_slice_in_dim(every_loss, my_place * tok_dev, tok_dev, 0)
    ordered = jnp.stack(
        [
            lax.dynamic_index_in_dim(log_total, batch_index ^ step, 0, keepdims=False)
            for step in range(batch_count)
        ]
    ).reshape(-1)

    mine = lax.dynamic_slice_in_dim(embedding, batch_index * own_rows, own_rows, 0)
    my_blocks = batch_index * own_blocks
    my_sampling = lax.dynamic_slice_in_dim(log_sampling, my_blocks, own_blocks, 0)
    my_allowed = lax.dynamic_slice_in_dim(allowed, my_blocks, own_blocks, 0)
    my_allowed = my_allowed.reshape(own_blocks, 1, -1)
    my_words = lax.dynamic_slice_in_dim(word_ids, my_blocks, own_blocks, 0)
    my_logits = lax.dot_general(
        mine, everyone, (((1,), (1,)), ((), ())), preferred_element_type=jnp.float32
    ).reshape(own_blocks, block_width, -1) - my_sampling[:, None, None]
    weights = jnp.where(my_allowed, jnp.exp(my_logits - ordered[None, None, :]), 0.0)
    hits = my_words[:, :, None] == target_ids.reshape(-1)[None, None, :]
    grad_logits = (weights - hits.astype(jnp.float32)).astype(jnp.bfloat16)
    grad_embed = lax.dot_general(
        grad_logits.reshape(own_rows, -1),
        everyone,
        (((1,), (0,)), ((), ())),
        preferred_element_type=jnp.float32,
    ).astype(jnp.bfloat16)
    return (token_loss, grad_embed)


def solution(mesh):
    in_specs = (P(("vocab", "batch"), None), P("vocab", None), P("vocab"), P(), P(), P())
    out_specs = (P(("vocab", "batch")), P(("vocab", "batch"), None))
    return jax.shard_map(body, mesh=mesh, in_specs=in_specs, out_specs=out_specs, check_vma=False)
```

time: 92.7 us -> 36.2 us (0.39)
  blocking collectives: 79.2 us -> 0 us
  starting transfers between devices: 3.33 us -> 13 us
  local copies, waits for them, and re-layouts: 2.52 us -> 8.75 us
  waiting for transfers between devices: 0.01 us -> 5.02 us
    all_gather x2 -> x0, blocking collectives: 40.8 us -> none  [the longest x1 32.5 us: body(): gathered = lax.all_gather(hidden, 'vocab', axis=0, tiled=True)]
    pmax x1 -> x0, blocking collectives: 21.3 us -> none  [body(): peak_value = lax.pmax(local_peak, 'vocab')]
    psum x1 -> x0, blocking collectives: 17.1 us -> none  [body(): denominator, target_logit = lax.psum((local_total, local_target), 'vocab')]
    all_to_all x1 -> x2, starting transfers between devices: 3.33 us -> 11.1 us  [the longest x1 8.31 us: body(): lax.all_to_all(copies, both, 0, 0, tiled=True, axis_index_groups=groups)]
    all_to_all x1 -> x2, waiting for transfers between devices: 0.01 us -> 4.67 us  [the longest x1 4.67 us: body(): stats = lax.all_to_all(stats, both, 0, 0, tiled=True)]
    ppermute x0 -> x3, starting transfers between devices: none -> 1.92 us  [body(): pieces.append(lax.ppermute(gathered, 'batch', pairs))]
    unnamed x2 -> x12, local copies, waits for them, and re-layouts: 0.01 us -> 1.84 us
    broadcast_in_dim x1 -> x5, local copies, waits for them, and re-layouts: 0.13 us -> 1.65 us  [the longest x1 1.53 us: body(): copies = jnp.broadcast_to(hidden[None], (vocab_count, tok_dev, width))]
  transfers between devices with their start and end apart: 1 -> 5, of which waited for: 0 -> 2; matrix products, arithmetic and copies ran while one was open for 1% -> 31% of each run, Pallas kernels for 0% -> 0%
where the time goes in v1:
time: 36.2 us; the launch traced here: 35.7 us
  starting transfers between devices  13 us (36%)
  local copies, waits for them, and re-layouts  8.75 us (24%)
  waiting for transfers between devices  5.02 us (14%)
  other arithmetic  4.99 us (14%)
  matrix products  2.47 us (7%)
  between operations  1.52 us (4%)
    all_to_all x1, starting transfers between devices, body(): lax.all_to_all(copies, both, 0, 0, tiled=True, axis_index_groups=groups)  8.31 us
    all_to_all x1, waiting for transfers between devices, body(): stats = lax.all_to_all(stats, both, 0, 0, tiled=True)  4.67 us
    all_to_all x1, starting transfers between devices, body(): stats = lax.all_to_all(stats, both, 0, 0, tiled=True)  2.77 us
    ppermute x3, starting transfers between devices, body(): pieces.append(lax.ppermute(gathered, 'batch', pairs))  1.92 us
    unnamed x12, local copies, waits for them, and re-layouts  1.84 us
    dot_general x1, matrix products, body(): lax.dot_general(grad_logits.reshape(own_rows, -1), everyone, (((1,), (0,)...  1.61 us
    broadcast_in_dim x1, local copies, waits for them, and re-layouts, body(): copies = jnp.broadcast_to(hidden[None], (vocab_count, tok_dev, width))  1.53 us
    reduce_sum x1, other arithmetic, body(): jnp.sum(jnp.where(places == vocab_index, jnp.arange(vocab_count), 0))  1.38 us
  transfers between devices with their start and end apart: 5, of which 2 were waited for; matrix products, arithmetic and copies ran while one was open for 31% of the time, Pallas kernels for 0%

profile of v1, /device:TPU:0, one launch (start us, length us, event | category | flops | bytes accessed | tf_op | source)
XLA Modules:
  0.0 35.7 jit_solution(17811107951294598955)
XLA Ops:
  0.6 1.5 %broadcast_in_dim.74 = bf16[8,8,1024]{2,1,0:T(8,128)(2,1)} broadcast(bf16[8,1024]{1,0:T(8,128)(2,1)} %param.7), dimensions={1,2} | broadcast | bytes 147456 | tf_op jit(solution)/shard_map/broadcast_in_dim | solution.py:32
  2.2 8.3 %all-to-all-start = ((bf16[8,8,1024]{2,1,0:T(8,128)(2,1)}), bf16[8,8,1024]{2,1,0:T(8,128)(2,1)S(1)}, u32[]{:S(2)}, u32[]{:S(2)}) async-start(bf16[8,8,1024]{2,1,0:T(8,128)(2,1)} %broadcast_in_dim.74), calls=%async_computation | async-start | bytes 262144 | tf_op jit(solution)/shard_map/all_to_all | solution.py:33
  10.5 1.4 %fusion.34 = s32[]{:T(128)} fusion(s32[8]{0:T(128)} %constant.93.clone, s32[]{:T(128)S(6)} %axis_index.23), kind=kLoop, calls=%fused_computation.69 | loop fusion | flops 23 | bytes 40 | tf_op jit(solution)/shard_map/reduce_sum | solution.py:87
  11.9 0.7 %convert_log_fusion = f32[8]{0:T(128)S(1)} fusion(s32[8]{0:T(128)} %param.9), kind=kLoop, calls=%fused_computation.71 | loop fusion | flops 8 | bytes 64 | tf_op jit(solution)/shard_map/log | solution.py:62
  12.7 0.7 %compare_select_fusion = s32[4]{0:T(128)S(1)} fusion(s32[4]{0:T(128)} %param.11), kind=kLoop, calls=%fused_computation.49 | loop fusion | flops 12 | bytes 32 | tf_op jit(solution)/shard_map/select_n | solution.py:57
  13.4 1.0 %fusion.41 = (s32[32]{0:T(128)S(1)}, s32[32]{0:T(128)S(1)}, s32[32]{0:T(128)S(1)}, s32[32]{0:T(128)S(1)}, s32[32]{0:T(128)S(1)}, /*index=5*/s32[32]{0:T(128)S(1)}, s32[32]{0:T(128)S(1)}, s32[32]{0:T(128)S(1)}) fusion(s32[256]{0:T(256)} %param.12), kind=kLoop, calls=%fused_computation.80 | loop fusion | bytes 2048 | tf_op jit(solution)/shard_map/slice | solution.py:48
  15.1 0.7 %add_multiply_fusion = s32[4,8]{1,0:T(4,128)S(1)} fusion(s32[4]{0:T(128)S(1)} %iota_xor_fusion, s32[8]{0:T(128)} %constant.95), kind=kLoop, calls=%fused_computation.65 | loop fusion | flops 64 | bytes 176 | tf_op jit(solution)/shard_map/mul | solution.py:44
  16.1 0.9 %copy.23 = s32[200,64]{1,0:T(8,128)S(1)} copy(s32[200,64]{0,1:T(8,128)} %param.10) | data formatting | bytes 102400 | tf_op args[3]
  17.1 0.6 %gather_fusion = s32[4,64]{1,0:T(4,128)S(1)} fusion(s32[200,64]{1,0:T(8,128)S(1)} %copy.23, s32[1024]{0:T(1024)S(1)} %pad_clamp_fusion), kind=kCustom, calls=%fused_computation | custom fusion | bytes 2064 | tf_op jit(solution)/shard_map/gather | solution.py:57
  17.7 0.2 compare_reduce_fusion
  18.0 0.5 %broadcast.141 = s32[]{:T(128)} broadcast(s32[]{:T(128)} %constant.71.clone.1), dimensions={} | broadcast | bytes 8 | tf_op jit(solution)/shard_map/jit(dynamic_index_in_dim)/dynamic_slice | solution.py:51
  18.5 0.7 %constant_dynamic-slice_fusion.2 = (s32[1,8,8]{2,0,1:T(1,128)S(1)}, s32[1,8,8]{2,0,1:T(1,128)S(1)}, s32[1,8,8]{2,0,1:T(1,128)S(1)}, s32[8,8]{1,0:T(8,128)S(1)}, s32[1,8,8]{2,0,1:T(1,128)S(1)}) fusion(s32[4,8,8]{2,0,1:T(4,128)S(1)} %constant_dynamic-update-slice_fusion, s32[]{:T(128)S(6)} %select_n.78, s32[]{:T(128)S(6)} %select_n.80, s32[]{:T(128)S(6)} %select_n.79, ...), kind=kLoop, calls=%fused_computation.52 | loop fusion | bytes 2324 | tf_op jit(solution)/shard_map/jit(dynamic_index_in_dim)/dynamic_slice | solution.py:51
  19.3 0.9 %select_reduce_fusion.2 = (f32[64]{0:T(128)S(1)}, f32[8,128,64]{1,2,0:T(8,128)S(1)}) fusion(pred[8,64]{1,0:T(8,128)(4,1)S(1)} %slice_bitcast_fusion, f32[8]{0:T(128)S(1)} %convert_log_fusion, bf16[8,128,1024]{2,1,0:T(8,128)(2,1)S(1)} %bitcast.27, bf16[8,8,1024]{2,1,0:T(8,128)(2,1)S(1)} %all-to-all-done), kind=kOutput, calls=%fused_computation.20 | convolution fusion | flops 134414272 | bytes 2491168 | tf_op jit(solution)/shard_map/dot_general | solution.py:65
  20.2 0.3 select_reduce_fusion
  20.5 0.8 %reshape.233 = f32[32,1,512]{2,1,0:T(1,128)} reshape(f32[32,8,64]{2,1,0:T(8,128)S(1)} %broadcast_in_dim.77) | data formatting | bytes 131072
  21.2 2.8 %all-to-all-start.1 = ((f32[32,1,512]{2,1,0:T(1,128)}), f32[32,1,512]{2,1,0:T(1,128)S(1)}, u32[]{:S(2)}, u32[]{:S(2)}) async-start(f32[32,1,512]{2,1,0:T(1,128)} %reshape.233), calls=%async_computation.1 | async-start | bytes 131072 | tf_op jit(solution)/shard_map/all_to_all | solution.py:80
  24.9 1.5 %collective-permute-start.2 = (bf16[64,1024]{1,0:T(8,128)(2,1)S(1)}, bf16[64,1024]{1,0:T(8,128)(2,1)S(1)}, u32[]{:S(2)}, u32[]{:S(2)}) collective-permute-start(bf16[64,1024]{1,0:T(8,128)(2,1)S(1)} %bitcast.28), channel_id=1, source_target_pairs={{0,3},{1,2},{2,1},{3,0},{4,7},{5,6},{6,5},{7,4},{8,11},{9,10},{10,... | collective-permute-start | bytes 393224 | tf_op jit(solution)/shard_map/ppermute | solution.py:38
  26.5 0.4 %collective-permute-start.1 = (bf16[64,1024]{1,0:T(8,128)(2,1)S(1)}, bf16[64,1024]{1,0:T(8,128)(2,1)S(1)}, u32[]{:S(2)}, u32[]{:S(2)}) collective-permute-start(bf16[64,1024]{1,0:T(8,128)(2,1)S(1)} %bitcast.29), channel_id=1, source_target_pairs={{0,2},{1,3},{2,0},{3,1},{4,6},{5,7},{6,4},{7,5},{8,10},{9,11},{10,... | collective-permute-start | bytes 393224 | tf_op jit(solution)/shard_map/ppermute | solution.py:38
  26.9 4.7 %all-to-all-done.1 = f32[32,1,512]{2,1,0:T(1,128)S(1)} async-done(((f32[32,1,512]{2,1,0:T(1,128)}), f32[32,1,512]{2,1,0:T(1,128)S(1)}, u32[]{:S(2)}, u32[]{:S(2)}) %all-to-all-start.1) | async-done | bytes 65568 | tf_op jit(solution)/shard_map/all_to_all | solution.py:80
  31.5 0.5 %broadcast.142 = f32[]{:T(128)} broadcast(f32[]{:T(128)} %constant.175), dimensions={} | broadcast | bytes 8 | tf_op jit(solution)/shard_map/all_to_all | solution.py:80
  32.0 0.8 %reduce.7 = f32[32,512]{1,0:T(8,128)S(1)} reduce(f32[32,1,512]{2,1,0:T(1,128)S(1)} %all-to-all-done.1, f32[]{:T(128)} %broadcast.142), dimensions={1}, to_apply=%all_to_all.7.reduce_sub_computation | reduce | bytes 131076 | tf_op jit(solution)/shard_map/all_to_all | solution.py:80
  33.2 0.6 %dynamic-slice_bitcast_fusion = f32[8]{0:T(128)} fusion(f32[4,64]{1,0:T(4,128)S(1)} %get-tuple-element.4, s32[]{:T(128)S(6)} %select_n.72, s32[]{:T(128)S(6)} %select_n.75), kind=kLoop, calls=%fused_computation.70 | loop fusion | bytes 72 | tf_op jit(solution)/shard_map/dynamic_slice | solution.py:88
  33.8 0.3 collective-permute-done.1
  34.1 1.6 %convolution_convert_fusion = bf16[256,1024]{1,0:T(8,128)(2,1)} fusion(pred[256,256]{1,0:T(32,128)(4,1)S(1)} %bitcast.35, bf16[64,1024]{1,0:T(8,128)(2,1)S(1)} %collective-permute-done.2, bf16[64,1024]{1,0:T(8,128)(2,1)S(1)} %collective-permute-done.1, bf16[64,1024]{1,0:T(8,128)(2,1)S(1)} %collective-permute-done, bf16[64,1024]{1,0:T(8,128)(2,1)S(1)} %bitcast.31, ...), kind=kOutput, calls=%fused_computation.1 | convolution fusion | flops 273350656 | bytes 2166788 | tf_op jit(solution)/shard_map/dot_general | solution.py:108
  (57 shorter events, 1.9 us)
Async XLA Ops:
  0.6 18.7 %copy-start = (bf16[1024,1024]{1,0:T(8,128)(2,1)S(1)}, bf16[1024,1024]{1,0:T(8,128)(2,1)}, u32[]{:S(2)}) copy-start(bf16[1024,1024]{1,0:T(8,128)(2,1)} %param.8) | copy-start | bytes 6291460
  2.2 17.1 %all-to-all-start = ((bf16[8,8,1024]{2,1,0:T(8,128)(2,1)}), bf16[8,8,1024]{2,1,0:T(8,128)(2,1)S(1)}, u32[]{:S(2)}, u32[]{:S(2)}) async-start(bf16[8,8,1024]{2,1,0:T(8,128)(2,1)} %broadcast_in_dim.74), calls=%async_computation | async-start | bytes 262144 | tf_op jit(solution)/shard_map/all_to_all | solution.py:33
  21.2 10.3 %all-to-all-start.1 = ((f32[32,1,512]{2,1,0:T(1,128)}), f32[32,1,512]{2,1,0:T(1,128)S(1)}, u32[]{:S(2)}, u32[]{:S(2)}) async-start(f32[32,1,512]{2,1,0:T(1,128)} %reshape.233), calls=%async_computation.1 | async-start | bytes 131072 | tf_op jit(solution)/shard_map/all_to_all | solution.py:80
  24.9 8.8 %collective-permute-start.2 = (bf16[64,1024]{1,0:T(8,128)(2,1)S(1)}, bf16[64,1024]{1,0:T(8,128)(2,1)S(1)}, u32[]{:S(2)}, u32[]{:S(2)}) collective-permute-start(bf16[64,1024]{1,0:T(8,128)(2,1)S(1)} %bitcast.28), channel_id=1, source_target_pairs={{0,3},{1,2},{2,1},{3,0},{4,7},{5,6},{6,5},{7,4},{8,11},{9,10},{10,... | collective-permute-start | bytes 393224 | tf_op jit(solution)/shard_map/ppermute | solution.py:38
  26.5 7.6 %collective-permute-start.1 = (bf16[64,1024]{1,0:T(8,128)(2,1)S(1)}, bf16[64,1024]{1,0:T(8,128)(2,1)S(1)}, u32[]{:S(2)}, u32[]{:S(2)}) collective-permute-start(bf16[64,1024]{1,0:T(8,128)(2,1)S(1)} %bitcast.29), channel_id=1, source_target_pairs={{0,2},{1,3},{2,0},{3,1},{4,6},{5,7},{6,4},{7,5},{8,10},{9,11},{10,... | collective-permute-start | bytes 393224 | tf_op jit(solution)/shard_map/ppermute | solution.py:38
  26.9 7.3 %collective-permute-start = (bf16[64,1024]{1,0:T(8,128)(2,1)S(1)}, bf16[64,1024]{1,0:T(8,128)(2,1)S(1)}, u32[]{:S(2)}, u32[]{:S(2)}) collective-permute-start(bf16[64,1024]{1,0:T(8,128)(2,1)S(1)} %bitcast.30), channel_id=1, source_target_pairs={{0,1},{1,0},{2,3},{3,2},{4,5},{5,4},{6,7},{7,6},{8,9},{9,8},{10,11... | collective-permute-start | bytes 393224 | tf_op jit(solution)/shard_map/ppermute | solution.py:38

commit v2 on v1

--- a/solution.py
+++ b/solution.py
@@ -1,9 +1,15 @@
+import functools
+
 import jax
 import jax.numpy as jnp
 from jax import lax
+from jax.experimental import pallas as pl
+from jax.experimental.pallas import tpu as pltpu
 from jax.sharding import PartitionSpec as P
 
 SEQ = 64
+LANES = 128
+KERNEL_VMEM = 8 * 1024 * 1024
 
 
 masked_fill = float(jnp.finfo(jnp.float32).min)
@@ -11,6 +17,253 @@
 
 def centre_first(count):
     return sorted(range(count), key=lambda i: (abs(i // 2 - count // 4), i // 2, -i))
+
+
+def iota(shape, axis):
+    return lax.broadcasted_iota(jnp.int32, shape, axis)
+
+
+def contract_last(a, b):
+    return lax.dot_general(a, b, (((1,), (1,)), ((), ())), preferred_element_type=jnp.float32)
+
+
+def prepare_kernel(
+    order, tok_dev, batch_count, sent_hbm, count_hbm, lists_hbm, targets_hbm, emb_hbm,
+    bias_ref, target_ref, kept_ref, sent_ref, count_ref, lists_ref, targets_ref, sems,
+):
+    sources = (sent_hbm, count_hbm, lists_hbm, targets_hbm, emb_hbm)
+    places = (sent_ref, count_ref, lists_ref, targets_ref, kept_ref)
+    fetches = [
+        pltpu.make_async_copy(src, dst, sems.at[i])
+        for i, (src, dst) in enumerate(zip(sources, places))
+    ]
+    for fetch in fetches:
+        fetch.start()
+    vocab_index = lax.axis_index("vocab")
+    batch_index = lax.axis_index("batch")
+    local_blocks, tokens = bias_ref.shape
+    group_tokens = tokens // batch_count
+    languages = lists_ref.shape[1]
+
+    lane = iota((1, tokens), 1)
+    source = batch_index ^ (lane // group_tokens)
+    position = (lane % group_tokens) // tok_dev
+    place = jnp.zeros((1, tokens), jnp.int32)
+    for j, v in enumerate(order):
+        place = jnp.where(position == j, v, place)
+    token = (place * batch_count + source) * tok_dev + lane % tok_dev
+    sentence = token // SEQ
+
+    for fetch in fetches[:-1]:
+        fetch.wait()
+    found = jnp.zeros((1, tokens), jnp.float32)
+    for start in range(0, tokens, LANES):
+        size = min(LANES, tokens - start)
+        part = targets_ref[:, start : start + size].astype(jnp.float32)
+        eye = iota((size, size), 0) == iota((size, size), 1)
+        column = jnp.sum(jnp.where(eye, part, 0.0), axis=1, keepdims=True)
+        hit = (iota((size, tokens), 0) + start) == token
+        found = found + jnp.sum(jnp.where(hit, column, 0.0), axis=0, keepdims=True)
+    target_ref[...] = found.astype(jnp.int32)
+
+    block = iota((local_blocks, 1), 0)
+    member = jnp.zeros((local_blocks, languages), jnp.float32)
+    counts = jnp.zeros((local_blocks, 1), jnp.float32)
+    for k in range(local_blocks):
+        listed = jnp.where(lists_ref[...] == vocab_index * local_blocks + k, 1.0, 0.0)
+        listed = jnp.max(listed, axis=0, keepdims=True)
+        member = jnp.where(block == k, listed, member)
+        counts = jnp.where(block == k, count_ref[k].astype(jnp.float32), counts)
+    log_counts = jnp.log(counts)
+    bias = jnp.full((local_blocks, tokens), jnp.inf, jnp.float32)
+    language = iota((local_blocks, languages), 1)
+    for s in range(sent_ref.shape[0]):
+        picked = jnp.where(language == sent_ref[s], member, 0.0)
+        picked = jnp.max(picked, axis=1, keepdims=True)
+        bias = jnp.where((sentence == s) & (picked > 0.5), log_counts, bias)
+    bias_ref[...] = bias
+    fetches[-1].wait()
+
+
+def stats_kernel(bias_ref, target_ref, emb_ref, rows_ref, stats_ref, logits_ref):
+    vocab_index = lax.axis_index("vocab")
+    group_tokens = rows_ref.shape[0]
+    local_rows = emb_ref.shape[0]
+    local_blocks = bias_ref.shape[0]
+    block_width = local_rows // local_blocks
+
+    raw = contract_last(emb_ref[...], rows_ref[...])
+    own_target = target_ref[:, :group_tokens] - vocab_index * local_rows
+    top = jnp.full((block_width, group_tokens), -jnp.inf, jnp.float32)
+    aimed = jnp.zeros((block_width, group_tokens), jnp.float32)
+    for k in range(local_blocks):
+        rows = slice(k * block_width, (k + 1) * block_width)
+        cell = bias_ref[k : k + 1, :group_tokens]
+        logits = jnp.where(cell < jnp.inf, raw[rows] - cell, -jnp.inf)
+        logits_ref[rows, :] = logits
+        top = jnp.maximum(top, logits)
+        word = iota((block_width, group_tokens), 0) + k * block_width
+        aimed = jnp.where(word == own_target, logits, aimed)
+    peak = jnp.maximum(jnp.max(top, axis=0, keepdims=True), masked_fill)
+    total = jnp.zeros((block_width, group_tokens), jnp.float32)
+    for k in range(local_blocks):
+        rows = slice(k * block_width, (k + 1) * block_width)
+        total = total + jnp.exp(logits_ref[rows, :] - peak)
+    total = jnp.sum(total, axis=0, keepdims=True)
+    aimed = jnp.sum(aimed, axis=0, keepdims=True)
+    row = iota((8, group_tokens), 0)
+    packed = jnp.where(row == 0, peak, jnp.where(row == 1, total, aimed))
+    for p in range(stats_ref.shape[0]):
+        for start in range(0, LANES, group_tokens):
+            stats_ref[p, :, start : start + group_tokens] = packed
+
+
+def grad_kernel(
+    order, tok_dev, batch_count, stats_ref, bias_ref, target_ref, emb_ref, *refs
+):
+    row_refs = refs[:batch_count]
+    loss_ref, grad_ref, weight_ref, everyone_ref = refs[batch_count:]
+    vocab_index = lax.axis_index("vocab")
+    batch_index = lax.axis_index("batch")
+    group_tokens = row_refs[0].shape[0]
+    own_rows = grad_ref.shape[0]
+    local_blocks = bias_ref.shape[0]
+    local_rows = emb_ref.shape[0]
+    block_width = local_rows // local_blocks
+    own_blocks = own_rows // block_width
+    vocab_count = stats_ref.shape[0] // batch_count
+
+    for m in range(batch_count):
+        everyone_ref[m * group_tokens : (m + 1) * group_tokens, :] = row_refs[m][...]
+    mine = emb_ref[pl.ds(pl.multiple_of(batch_index * own_rows, own_rows), own_rows), :]
+    raw = contract_last(mine, everyone_ref[...])
+    biases = [bias_ref[pl.ds(batch_index * own_blocks + k, 1), :] for k in range(own_blocks)]
+
+    for m in range(batch_count):
+        group = batch_index ^ m
+        parts = [stats_ref[v * batch_count + group] for v in range(vocab_count)]
+        peak = parts[0][0:1]
+        for part in parts[1:]:
+            peak = jnp.maximum(peak, part[0:1])
+        total = jnp.zeros_like(peak)
+        for part in parts:
+            total = total + part[1:2] * jnp.exp(part[0:1] - peak)
+        log_total = (peak + jnp.log(total))[:, :group_tokens]
+        if m == 0:
+            aimed = jnp.zeros_like(peak)
+            for part in parts:
+                aimed = aimed + part[2:3]
+            loss = log_total - aimed[:, :group_tokens]
+            my_place = jnp.int32(0)
+            for j, v in enumerate(order):
+                my_place = jnp.where(vocab_index == v, j, my_place)
+            wanted = my_place * tok_dev + iota((tok_dev, group_tokens), 0)
+            chosen = jnp.where(iota((tok_dev, group_tokens), 1) == wanted, loss, 0.0)
+            chosen = jnp.sum(chosen, axis=1, keepdims=True)
+            eye = iota((tok_dev, tok_dev), 0) == iota((tok_dev, tok_dev), 1)
+            loss_ref[...] = jnp.sum(jnp.where(eye, chosen, 0.0), axis=0, keepdims=True)
+        lanes = slice(m * group_tokens, (m + 1) * group_tokens)
+        target = target_ref[:, lanes] - vocab_index * local_rows - batch_index * own_rows
+        for k in range(own_blocks):
+            rows = slice(k * block_width, (k + 1) * block_width)
+            cell = biases[k][:, lanes]
+            logits = raw[rows, lanes] - cell
+            weight = jnp.where(cell < jnp.inf, jnp.exp(logits - log_total), 0.0)
+            word = iota((block_width, group_tokens), 0) + k * block_width
+            weight = weight - jnp.where(word == target, 1.0, 0.0)
+            weight_ref[rows, lanes] = weight.astype(jnp.bfloat16)
+    grad_ref[...] = jnp.dot(
+        weight_ref[...], everyone_ref[...], preferred_element_type=jnp.float32
+    ).astype(grad_ref.dtype)
+
+
+VMEM = pl.BlockSpec(memory_space=pltpu.VMEM)
+
+
+def fused_body(hidden, embedding, block_counts, lang_blocks, sent_lang, targets):
+    tok_dev, width = hidden.shape
+    vocab_count = lax.axis_size("vocab")
+    batch_count = lax.axis_size("batch")
+    local_rows = embedding.shape[0]
+    local_blocks = block_counts.shape[0]
+    own_rows = local_rows // batch_count
+    group_tokens = vocab_count * tok_dev
+    tokens = group_tokens * batch_count
+    devices = vocab_count * batch_count
+    order = centre_first(vocab_count)
+    both = ("vocab", "batch")
+    groups = [[v * batch_count + b for v in order] for b in range(batch_count)]
+    struct = jax.ShapeDtypeStruct
+
+    copies = jnp.broadcast_to(hidden[None], (vocab_count, tok_dev, width))
+    gathered = lax.all_to_all(copies, both, 0, 0, tiled=True, axis_index_groups=groups)
+    gathered = gathered.reshape(group_tokens, width)
+    pieces = [gathered]
+    for step in range(1, batch_count):
+        pairs = [(b, b ^ step) for b in range(batch_count)]
+        pieces.append(lax.ppermute(gathered, "batch", pairs))
+
+    limit = pltpu.CompilerParams(vmem_limit_bytes=KERNEL_VMEM)
+    bias, target_ids, kept = pl.pallas_call(
+        functools.partial(prepare_kernel, order, tok_dev, batch_count),
+        out_shape=(
+            struct((local_blocks, tokens), jnp.float32),
+            struct((1, tokens), jnp.int32),
+            struct(embedding.shape, embedding.dtype),
+        ),
+        in_specs=[pl.BlockSpec(memory_space=pltpu.HBM)] * 5,
+        out_specs=(VMEM, VMEM, VMEM),
+        scratch_shapes=[
+            pltpu.SMEM(sent_lang.shape, jnp.int32),
+            pltpu.SMEM(block_counts.shape, jnp.int32),
+            pltpu.VMEM(lang_blocks.shape[::-1], jnp.int32),
+            pltpu.VMEM((1, tokens), jnp.int32),
+            pltpu.SemaphoreType.DMA((5,)),
+        ],
+        compiler_params=limit,
+        name="prepare",
+        cost_estimate=pl.CostEstimate(
+            flops=tokens * tokens, bytes_accessed=4 * local_rows * width, transcendentals=0
+        ),
+    )(
+        *(
+            pltpu.with_memory_space_constraint(x, pltpu.HBM)
+            for x in (sent_lang, block_counts, lang_blocks.T, targets.reshape(1, -1), embedding)
+        )
+    )
+    stats = pl.pallas_call(
+        stats_kernel,
+        out_shape=struct((devices, 8, LANES), jnp.float32),
+        in_specs=[VMEM] * 4,
+        out_specs=VMEM,
+        scratch_shapes=[pltpu.VMEM((local_rows, group_tokens), jnp.float32)],
+        compiler_params=limit,
+        name="stats",
+        cost_estimate=pl.CostEstimate(
+            flops=2 * local_rows * group_tokens * width,
+            bytes_accessed=2 * local_rows * width,
+            transcendentals=local_rows * group_tokens,
+        ),
+    )(bias, target_ids, kept, gathered)
+    stats = lax.all_to_all(stats, both, 0, 0, tiled=True)
+    loss, grad = pl.pallas_call(
+        functools.partial(grad_kernel, order, tok_dev, batch_count),
+        out_shape=(struct((1, tok_dev), jnp.float32), struct((own_rows, width), jnp.bfloat16)),
+        in_specs=[VMEM] * (4 + batch_count),
+        out_specs=(VMEM, VMEM),
+        scratch_shapes=[
+            pltpu.VMEM((own_rows, tokens), jnp.bfloat16),
+            pltpu.VMEM((tokens, width), jnp.bfloat16),
+        ],
+        name="grad",
+        compiler_params=limit,
+        cost_estimate=pl.CostEstimate(
+            flops=4 * own_rows * tokens * width,
+            bytes_accessed=2 * own_rows * width,
+            transcendentals=own_rows * tokens,
+        ),
+    )(stats, bias, target_ids, kept, *pieces)
+    return (loss.reshape(tok_dev), grad)
 
 
 def body(hidden, embedding, block_counts, lang_blocks, sent_lang, targets):
@@ -117,4 +370,10 @@
 def solution(mesh):
     in_specs = (P(("vocab", "batch"), None), P("vocab", None), P("vocab"), P(), P(), P())
     out_specs = (P(("vocab", "batch")), P(("vocab", "batch"), None))
-    return jax.shard_map(body, mesh=mesh, in_specs=in_specs, out_specs=out_specs, check_vma=False)
+
+    def step(hidden, *rest):
+        group_tokens = hidden.shape[0] * lax.axis_size("vocab")
+        chosen = fused_body if LANES % group_tokens == 0 else body
+        return chosen(hidden, *rest)
+
+    return jax.shard_map(step, mesh=mesh, in_specs=in_specs, out_specs=out_specs, check_vma=False)

time: 36.2 us -> 33 us (0.912)
  local copies, waits for them, and re-layouts: 8.75 us -> 1.38 us
  waiting for transfers between devices: 5.02 us -> 10.1 us
  Pallas kernels: 0 us -> 4.99 us
  other arithmetic: 4.99 us -> 0 us
  starting transfers between devices: 13 us -> 15.5 us
  matrix products: 2.47 us -> 0 us
  between operations: 1.52 us -> 0.65 us
    ppermute x3, waiting for transfers between devices: 0.35 us -> 8.04 us  [fused_body(): pieces.append(lax.ppermute(gathered, 'batch', pairs))]
    pallas_call x0 -> x3, Pallas kernels: none -> 4.99 us  [the longest x1 1.78 us: fused_body(): pl.pallas_call(functools.partial(grad_kernel, order, tok_dev, batch_count...]
    all_to_all x2, waiting for transfers between devices: 4.67 us -> 2.02 us  [the longest x1 2.02 us: fused_body(): lax.all_to_all(copies, both, 0, 0, tiled=True, axis_index_groups=groups)]
    dot_general x2 -> x0, matrix products: 2.47 us -> none  [the longest x1 1.61 us: body(): lax.dot_general(grad_logits.reshape(own_rows, -1), everyone, (((1,), (0,)...]
    all_to_all x2, starting transfers between devices: 11.1 us -> 13.5 us  [the longest x1 8.31 us: fused_body(): lax.all_to_all(copies, both, 0, 0, tiled=True, axis_index_groups=groups)]
    dynamic_slice x7 -> x0, local copies, waits for them, and re-layouts: 1.88 us -> none  [the longest x2 1.19 us: body(): lax.dynamic_index_in_dim(target_table, batch_index ^ step, 0, keepdims=Fa...]
    unnamed x12 -> x0, local copies, waits for them, and re-layouts: 1.84 us -> none
    reduce_sum x3 -> x0, other arithmetic: 1.67 us -> none  [the longest x1 1.38 us: body(): jnp.sum(jnp.where(places == vocab_index, jnp.arange(vocab_count), 0))]
  transfers between devices with their start and end apart: 5 -> 5, of which waited for: 2 -> 3; matrix products, arithmetic and copies ran while one was open for 31% -> 0% of each run, Pallas kernels for 0% -> 5%
where the time goes in v2:
time: 33 us; the launch traced here: 32.6 us
  starting transfers between devices  15.5 us (47%)
  waiting for transfers between devices  10.1 us (31%)
  Pallas kernels  4.99 us (15%)
  local copies, waits for them, and re-layouts  1.38 us (4%)
  between operations  0.65 us (2%)
    all_to_all x1, starting transfers between devices, fused_body(): lax.all_to_all(copies, both, 0, 0, tiled=True, axis_index_groups=groups)  8.31 us
    ppermute x3, waiting for transfers between devices, fused_body(): pieces.append(lax.ppermute(gathered, 'batch', pairs))  8.04 us
    all_to_all x1, starting transfers between devices, fused_body(): stats = lax.all_to_all(stats, both, 0, 0, tiled=True)  5.21 us
    all_to_all x1, waiting for transfers between devices, fused_body(): lax.all_to_all(copies, both, 0, 0, tiled=True, axis_index_groups=groups)  2.02 us
    ppermute x3, starting transfers between devices, fused_body(): pieces.append(lax.ppermute(gathered, 'batch', pairs))  1.95 us
    pallas_call x1, Pallas kernels, fused_body(): pl.pallas_call(functools.partial(grad_kernel, order, tok_dev, batch_count...  1.78 us
    pallas_call x1, Pallas kernels, fused_body(): pl.pallas_call(functools.partial(prepare_kernel, order, tok_dev, batch_co...  1.69 us
    pallas_call x1, Pallas kernels, fused_body(): pl.pallas_call(stats_kernel, out_shape=struct((devices, 8, LANES), jnp.fl...  1.52 us
  transfers between devices with their start and end apart: 5, of which 3 were waited for; matrix products, arithmetic and copies ran while one was open for 0% of the time, Pallas kernels for 5%

profile of v2, /device:TPU:0, one launch (start us, length us, event | category | flops | bytes accessed | tf_op | source)
XLA Modules:
  0.0 32.6 jit_solution(17095106048582008654)
XLA Ops:
  0.6 1.4 %broadcast_in_dim.2 = bf16[8,8,1024]{2,1,0:T(8,128)(2,1)} broadcast(bf16[8,1024]{1,0:T(8,128)(2,1)} %param.6), dimensions={1,2} | broadcast | bytes 147456 | tf_op jit(solution)/shard_map/broadcast_in_dim | solution.py:198
  2.0 8.3 %all-to-all-start = ((bf16[8,8,1024]{2,1,0:T(8,128)(2,1)}), bf16[8,8,1024]{2,1,0:T(8,128)(2,1)S(1)}, u32[]{:S(2)}, u32[]{:S(2)}) async-start(bf16[8,8,1024]{2,1,0:T(8,128)(2,1)} %broadcast_in_dim.2), calls=%async_computation | async-start | bytes 262144 | tf_op jit(solution)/shard_map/all_to_all | solution.py:199
  10.3 1.7 %prepare.1 = (f32[8,256]{1,0:T(8,128)S(1)}, s32[1,256]{1,0:T(1,128)S(1)}, bf16[1024,1024]{1,0:T(8,128)(2,1)S(1)}) custom-call(s32[4]{0:T(128)} %sent_hbm.1, s32[8]{0:T(128)} %count_hbm.1, s32[64,200]{1,0:T(8,128)} %bitcast.9, s32[1,256]{1,0:T(1,128)} %bitcast.10, bf16[1024,1024]{1,0:T(8,128)(2,1)} %emb_hbm.1), custom_call_target="tpu_custom_call" | custom-call | flops 65536 | bytes 4194304 | tf_op jit(solution)/shard_map/prepare/pallas_call | solution.py:207
  12.0 2.0 %all-to-all-done = bf16[8,8,1024]{2,1,0:T(8,128)(2,1)S(1)} async-done(((bf16[8,8,1024]{2,1,0:T(8,128)(2,1)}), bf16[8,8,1024]{2,1,0:T(8,128)(2,1)S(1)}, u32[]{:S(2)}, u32[]{:S(2)}) %all-to-all-start) | async-done | bytes 131104 | tf_op jit(solution)/shard_map/all_to_all | solution.py:199
  14.0 1.5 %stats.1 = f32[32,8,128]{2,1,0:T(8,128)} custom-call(f32[8,256]{1,0:T(8,128)S(1)} %get-tuple-element.7.bias_ref, s32[1,256]{1,0:T(1,128)S(1)} %get-tuple-element.8.target_ref, bf16[1024,1024]{1,0:T(8,128)(2,1)S(1)} %get-tuple-element.9.emb_ref, bf16[64,1024]{1,0:T(8,128)(2,1)S(1)} %bitcast.4), custom_call_target="tpu_custom_call" | custom-call | flops 134217728 | bytes 2097152 | tf_op jit(solution)/shard_map/stats/pallas_call | solution.py:234
  15.6 5.2 %all-to-all-start.1 = ((f32[32,8,128]{2,1,0:T(8,128)}), f32[32,8,128]{2,1,0:T(8,128)S(1)}, u32[]{:S(2)}, u32[]{:S(2)}) async-start(f32[32,8,128]{2,1,0:T(8,128)} %stats.1), calls=%async_computation.1 | async-start | bytes 262144 | tf_op jit(solution)/shard_map/all_to_all | solution.py:248
  20.8 1.6 %collective-permute-start.2 = (bf16[64,1024]{1,0:T(8,128)(2,1)S(1)}, bf16[64,1024]{1,0:T(8,128)(2,1)S(1)}, u32[]{:S(2)}, u32[]{:S(2)}) collective-permute-start(bf16[64,1024]{1,0:T(8,128)(2,1)S(1)} %bitcast.5), channel_id=1, source_target_pairs={{0,3},{1,2},{2,1},{3,0},{4,7},{5,6},{6,5},{7,4},{8,11},{9,10},{10,... | collective-permute-start | bytes 393224 | tf_op jit(solution)/shard_map/ppermute | solution.py:204
  22.3 0.4 %collective-permute-start.1 = (bf16[64,1024]{1,0:T(8,128)(2,1)S(1)}, bf16[64,1024]{1,0:T(8,128)(2,1)S(1)}, u32[]{:S(2)}, u32[]{:S(2)}) collective-permute-start(bf16[64,1024]{1,0:T(8,128)(2,1)S(1)} %bitcast.6), channel_id=1, source_target_pairs={{0,2},{1,3},{2,0},{3,1},{4,6},{5,7},{6,4},{7,5},{8,10},{9,11},{10,... | collective-permute-start | bytes 393224 | tf_op jit(solution)/shard_map/ppermute | solution.py:204
  22.7 0.0 collective-permute-start
  22.7 4.4 %collective-permute-done.2.refs_3_ = bf16[64,1024]{1,0:T(8,128)(2,1)S(1)} collective-permute-done((bf16[64,1024]{1,0:T(8,128)(2,1)S(1)}, bf16[64,1024]{1,0:T(8,128)(2,1)S(1)}, u32[]{:S(2)}, u32[]{:S(2)}) %collective-permute-start.2) | collective-permute-done | bytes 131104 | tf_op jit(solution)/shard_map/ppermute | solution.py:204
  27.2 3.6 %collective-permute-done.1.refs_2_ = bf16[64,1024]{1,0:T(8,128)(2,1)S(1)} collective-permute-done((bf16[64,1024]{1,0:T(8,128)(2,1)S(1)}, bf16[64,1024]{1,0:T(8,128)(2,1)S(1)}, u32[]{:S(2)}, u32[]{:S(2)}) %collective-permute-start.1) | collective-permute-done | bytes 131104 | tf_op jit(solution)/shard_map/ppermute | solution.py:204
  30.8 0.0 collective-permute-done.refs_1_
  30.8 0.0 all-to-all-done.1.stats_ref
  30.8 1.8 %grad.1 = (f32[1,8]{1,0:T(1,128)}, bf16[256,1024]{1,0:T(8,128)(2,1)}) custom-call(f32[32,8,128]{2,1,0:T(8,128)S(1)} %all-to-all-done.1.stats_ref, f32[8,256]{1,0:T(8,128)S(1)} %get-tuple-element.7.bias_ref, s32[1,256]{1,0:T(1,128)S(1)} %get-tuple-element.8.target_ref, bf16[1024,1024]{1,0:T(8,128)(2,1)S(1)} %get-tuple-element.9.emb_ref, ...), custom_call_target="tpu_custom_call" | custom-call | flops 268435456 | bytes 524288 | tf_op jit(solution)/shard_map/grad/pallas_call | solution.py:249
Async XLA Ops:
  2.0 12.0 %all-to-all-start = ((bf16[8,8,1024]{2,1,0:T(8,128)(2,1)}), bf16[8,8,1024]{2,1,0:T(8,128)(2,1)S(1)}, u32[]{:S(2)}, u32[]{:S(2)}) async-start(bf16[8,8,1024]{2,1,0:T(8,128)(2,1)} %broadcast_in_dim.2), calls=%async_computation | async-start | bytes 262144 | tf_op jit(solution)/shard_map/all_to_all | solution.py:199
  15.6 15.2 %all-to-all-start.1 = ((f32[32,8,128]{2,1,0:T(8,128)}), f32[32,8,128]{2,1,0:T(8,128)S(1)}, u32[]{:S(2)}, u32[]{:S(2)}) async-start(f32[32,8,128]{2,1,0:T(8,128)} %stats.1), calls=%async_computation.1 | async-start | bytes 262144 | tf_op jit(solution)/shard_map/all_to_all | solution.py:248
  20.8 6.4 %collective-permute-start.2 = (bf16[64,1024]{1,0:T(8,128)(2,1)S(1)}, bf16[64,1024]{1,0:T(8,128)(2,1)S(1)}, u32[]{:S(2)}, u32[]{:S(2)}) collective-permute-start(bf16[64,1024]{1,0:T(8,128)(2,1)S(1)} %bitcast.5), channel_id=1, source_target_pairs={{0,3},{1,2},{2,1},{3,0},{4,7},{5,6},{6,5},{7,4},{8,11},{9,10},{10,... | collective-permute-start | bytes 393224 | tf_op jit(solution)/shard_map/ppermute | solution.py:204
  22.3 8.4 %collective-permute-start.1 = (bf16[64,1024]{1,0:T(8,128)(2,1)S(1)}, bf16[64,1024]{1,0:T(8,128)(2,1)S(1)}, u32[]{:S(2)}, u32[]{:S(2)}) collective-permute-start(bf16[64,1024]{1,0:T(8,128)(2,1)S(1)} %bitcast.6), channel_id=1, source_target_pairs={{0,2},{1,3},{2,0},{3,1},{4,6},{5,7},{6,4},{7,5},{8,10},{9,11},{10,... | collective-permute-start | bytes 393224 | tf_op jit(solution)/shard_map/ppermute | solution.py:204
  22.7 8.0 %collective-permute-start = (bf16[64,1024]{1,0:T(8,128)(2,1)S(1)}, bf16[64,1024]{1,0:T(8,128)(2,1)S(1)}, u32[]{:S(2)}, u32[]{:S(2)}) collective-permute-start(bf16[64,1024]{1,0:T(8,128)(2,1)S(1)} %bitcast.7), channel_id=1, source_target_pairs={{0,1},{1,0},{2,3},{3,2},{4,5},{5,4},{6,7},{7,6},{8,9},{9,8},{10,11... | collective-permute-start | bytes 393224 | tf_op jit(solution)/shard_map/ppermute | solution.py:204

commit v3 on v2

--- a/solution.py
+++ b/solution.py
@@ -199,9 +199,12 @@
     gathered = lax.all_to_all(copies, both, 0, 0, tiled=True, axis_index_groups=groups)
     gathered = gathered.reshape(group_tokens, width)
     pieces = [gathered]
-    for step in range(1, batch_count):
+    step = batch_count // 2
+    while step:
         pairs = [(b, b ^ step) for b in range(batch_count)]
-        pieces.append(lax.ppermute(gathered, "batch", pairs))
+        received = [lax.ppermute(piece, "batch", pairs) for piece in pieces]
+        pieces = [half for pair in zip(pieces, received) for half in pair]
+        step //= 2
 
     limit = pltpu.CompilerParams(vmem_limit_bytes=KERNEL_VMEM)
     bias, target_ids, kept = pl.pallas_call(

time: 33 us -> 31.7 us (0.961)
  starting transfers between devices: 15.5 us -> 14.7 us
  waiting for transfers between devices: 10.1 us -> 9.65 us
    ppermute x3, waiting for transfers between devices: 8.04 us -> 0.84 us  [fused_body(): received = [lax.ppermute(piece, 'batch', pairs) for piece in pieces]]
    all_to_all x1, waiting for transfers between devices: 0.01 us -> 6.79 us  [fused_body(): stats = lax.all_to_all(stats, both, 0, 0, tiled=True)]
    all_to_all x1, starting transfers between devices: 5.21 us -> 4.26 us  [fused_body(): stats = lax.all_to_all(stats, both, 0, 0, tiled=True)]
  transfers between devices with their start and end apart: 5 -> 5, of which waited for: 3 -> 3; matrix products, arithmetic and copies ran while one was open for 0% -> 0% of each run, Pallas kernels for 5% -> 10%
where the time goes in v3:
time: 31.7 us; the launch traced here: 31.3 us
  starting transfers between devices  14.7 us (46%)
  waiting for transfers between devices  9.65 us (30%)
  Pallas kernels  4.98 us (16%)
  local copies, waits for them, and re-layouts  1.38 us (4%)
  between operations  0.65 us (2%)
    all_to_all x1, starting transfers between devices, fused_body(): lax.all_to_all(copies, both, 0, 0, tiled=True, axis_index_groups=groups)  8.31 us
    all_to_all x1, waiting for transfers between devices, fused_body(): stats = lax.all_to_all(stats, both, 0, 0, tiled=True)  6.79 us
    all_to_all x1, starting transfers between devices, fused_body(): stats = lax.all_to_all(stats, both, 0, 0, tiled=True)  4.26 us
    ppermute x3, starting transfers between devices, fused_body(): received = [lax.ppermute(piece, 'batch', pairs) for piece in pieces]  2.1 us
    all_to_all x1, waiting for transfers between devices, fused_body(): lax.all_to_all(copies, both, 0, 0, tiled=True, axis_index_groups=groups)  2.02 us
    pallas_call x1, Pallas kernels, fused_body(): pl.pallas_call(functools.partial(grad_kernel, order, tok_dev, batch_count...  1.78 us
    pallas_call x1, Pallas kernels, fused_body(): pl.pallas_call(functools.partial(prepare_kernel, order, tok_dev, batch_co...  1.69 us
    pallas_call x1, Pallas kernels, fused_body(): pl.pallas_call(stats_kernel, out_shape=struct((devices, 8, LANES), jnp.fl...  1.52 us
  transfers between devices with their start and end apart: 5, of which 3 were waited for; matrix products, arithmetic and copies ran while one was open for 0% of the time, Pallas kernels for 10%

profile of v3, /device:TPU:0, one launch (start us, length us, event | category | flops | bytes accessed | tf_op | source)
XLA Modules:
  0.0 31.3 jit_solution(9936236032902131696)
XLA Ops:
  0.6 1.4 %broadcast_in_dim.2 = bf16[8,8,1024]{2,1,0:T(8,128)(2,1)} broadcast(bf16[8,1024]{1,0:T(8,128)(2,1)} %param.6), dimensions={1,2} | broadcast | bytes 147456 | tf_op jit(solution)/shard_map/broadcast_in_dim | solution.py:198
  2.0 8.3 %all-to-all-start = ((bf16[8,8,1024]{2,1,0:T(8,128)(2,1)}), bf16[8,8,1024]{2,1,0:T(8,128)(2,1)S(1)}, u32[]{:S(2)}, u32[]{:S(2)}) async-start(bf16[8,8,1024]{2,1,0:T(8,128)(2,1)} %broadcast_in_dim.2), calls=%async_computation | async-start | bytes 262144 | tf_op jit(solution)/shard_map/all_to_all | solution.py:199
  10.3 1.7 %prepare.1 = (f32[8,256]{1,0:T(8,128)S(1)}, s32[1,256]{1,0:T(1,128)S(1)}, bf16[1024,1024]{1,0:T(8,128)(2,1)S(1)}) custom-call(s32[4]{0:T(128)} %sent_hbm.1, s32[8]{0:T(128)} %count_hbm.1, s32[64,200]{1,0:T(8,128)} %bitcast.8, s32[1,256]{1,0:T(1,128)} %bitcast.9, bf16[1024,1024]{1,0:T(8,128)(2,1)} %emb_hbm.1), custom_call_target="tpu_custom_call" | custom-call | flops 65536 | bytes 4194304 | tf_op jit(solution)/shard_map/prepare/pallas_call | solution.py:210
  12.0 2.0 %all-to-all-done = bf16[8,8,1024]{2,1,0:T(8,128)(2,1)S(1)} async-done(((bf16[8,8,1024]{2,1,0:T(8,128)(2,1)}), bf16[8,8,1024]{2,1,0:T(8,128)(2,1)S(1)}, u32[]{:S(2)}, u32[]{:S(2)}) %all-to-all-start) | async-done | bytes 131104 | tf_op jit(solution)/shard_map/all_to_all | solution.py:199
  14.0 1.5 %collective-permute-start.1 = (bf16[64,1024]{1,0:T(8,128)(2,1)S(1)}, bf16[64,1024]{1,0:T(8,128)(2,1)S(1)}, u32[]{:S(2)}, u32[]{:S(2)}) collective-permute-start(bf16[64,1024]{1,0:T(8,128)(2,1)S(1)} %bitcast.4), channel_id=1, source_target_pairs={{0,2},{1,3},{2,0},{3,1},{4,6},{5,7},{6,4},{7,5},{8,10},{9,11},{10,... | collective-permute-start | bytes 393224 | tf_op jit(solution)/shard_map/ppermute | solution.py:205
  15.6 1.5 %stats.1 = f32[32,8,128]{2,1,0:T(8,128)} custom-call(f32[8,256]{1,0:T(8,128)S(1)} %get-tuple-element.7.bias_ref, s32[1,256]{1,0:T(1,128)S(1)} %get-tuple-element.8.target_ref, bf16[1024,1024]{1,0:T(8,128)(2,1)S(1)} %get-tuple-element.9.emb_ref, bf16[64,1024]{1,0:T(8,128)(2,1)S(1)} %bitcast.5), custom_call_target="tpu_custom_call" | custom-call | flops 134217728 | bytes 2097152 | tf_op jit(solution)/shard_map/stats/pallas_call | solution.py:237
  17.1 4.3 %all-to-all-start.1 = ((f32[32,8,128]{2,1,0:T(8,128)}), f32[32,8,128]{2,1,0:T(8,128)S(1)}, u32[]{:S(2)}, u32[]{:S(2)}) async-start(f32[32,8,128]{2,1,0:T(8,128)} %stats.1), calls=%async_computation.1 | async-start | bytes 262144 | tf_op jit(solution)/shard_map/all_to_all | solution.py:251
  21.3 0.3 %collective-permute-start = (bf16[64,1024]{1,0:T(8,128)(2,1)S(1)}, bf16[64,1024]{1,0:T(8,128)(2,1)S(1)}, u32[]{:S(2)}, u32[]{:S(2)}) collective-permute-start(bf16[64,1024]{1,0:T(8,128)(2,1)S(1)} %bitcast.6), channel_id=1, source_target_pairs={{0,1},{1,0},{2,3},{3,2},{4,5},{5,4},{6,7},{7,6},{8,9},{9,8},{10,11... | collective-permute-start | bytes 393224 | tf_op jit(solution)/shard_map/ppermute | solution.py:205
  21.7 0.0 collective-permute-done.1.refs_2_
  21.7 0.3 collective-permute-start.2
  21.9 0.8 %collective-permute-done.refs_1_ = bf16[64,1024]{1,0:T(8,128)(2,1)S(1)} collective-permute-done((bf16[64,1024]{1,0:T(8,128)(2,1)S(1)}, bf16[64,1024]{1,0:T(8,128)(2,1)S(1)}, u32[]{:S(2)}, u32[]{:S(2)}) %collective-permute-start) | collective-permute-done | bytes 131104 | tf_op jit(solution)/shard_map/ppermute | solution.py:205
  22.8 6.8 %all-to-all-done.1.stats_ref = f32[32,8,128]{2,1,0:T(8,128)S(1)} async-done(((f32[32,8,128]{2,1,0:T(8,128)}), f32[32,8,128]{2,1,0:T(8,128)S(1)}, u32[]{:S(2)}, u32[]{:S(2)}) %all-to-all-start.1) | async-done | bytes 131104 | tf_op jit(solution)/shard_map/all_to_all | solution.py:251
  29.5 0.0 collective-permute-done.2.refs_3_
  29.5 1.8 %grad.1 = (f32[1,8]{1,0:T(1,128)}, bf16[256,1024]{1,0:T(8,128)(2,1)}) custom-call(f32[32,8,128]{2,1,0:T(8,128)S(1)} %all-to-all-done.1.stats_ref, f32[8,256]{1,0:T(8,128)S(1)} %get-tuple-element.7.bias_ref, s32[1,256]{1,0:T(1,128)S(1)} %get-tuple-element.8.target_ref, bf16[1024,1024]{1,0:T(8,128)(2,1)S(1)} %get-tuple-element.9.emb_ref, ...), custom_call_target="tpu_custom_call" | custom-call | flops 268435456 | bytes 524288 | tf_op jit(solution)/shard_map/grad/pallas_call | solution.py:252
Async XLA Ops:
  2.0 12.0 %all-to-all-start = ((bf16[8,8,1024]{2,1,0:T(8,128)(2,1)}), bf16[8,8,1024]{2,1,0:T(8,128)(2,1)S(1)}, u32[]{:S(2)}, u32[]{:S(2)}) async-start(bf16[8,8,1024]{2,1,0:T(8,128)(2,1)} %broadcast_in_dim.2), calls=%async_computation | async-start | bytes 262144 | tf_op jit(solution)/shard_map/all_to_all | solution.py:199
  14.0 7.6 %collective-permute-start.1 = (bf16[64,1024]{1,0:T(8,128)(2,1)S(1)}, bf16[64,1024]{1,0:T(8,128)(2,1)S(1)}, u32[]{:S(2)}, u32[]{:S(2)}) collective-permute-start(bf16[64,1024]{1,0:T(8,128)(2,1)S(1)} %bitcast.4), channel_id=1, source_target_pairs={{0,2},{1,3},{2,0},{3,1},{4,6},{5,7},{6,4},{7,5},{8,10},{9,11},{10,... | collective-permute-start | bytes 393224 | tf_op jit(solution)/shard_map/ppermute | solution.py:205
  17.1 12.5 %all-to-all-start.1 = ((f32[32,8,128]{2,1,0:T(8,128)}), f32[32,8,128]{2,1,0:T(8,128)S(1)}, u32[]{:S(2)}, u32[]{:S(2)}) async-start(f32[32,8,128]{2,1,0:T(8,128)} %stats.1), calls=%async_computation.1 | async-start | bytes 262144 | tf_op jit(solution)/shard_map/all_to_all | solution.py:251
  21.3 1.4 %collective-permute-start = (bf16[64,1024]{1,0:T(8,128)(2,1)S(1)}, bf16[64,1024]{1,0:T(8,128)(2,1)S(1)}, u32[]{:S(2)}, u32[]{:S(2)}) collective-permute-start(bf16[64,1024]{1,0:T(8,128)(2,1)S(1)} %bitcast.6), channel_id=1, source_target_pairs={{0,1},{1,0},{2,3},{3,2},{4,5},{5,4},{6,7},{7,6},{8,9},{9,8},{10,11... | collective-permute-start | bytes 393224 | tf_op jit(solution)/shard_map/ppermute | solution.py:205
  21.7 7.9 %collective-permute-start.2 = (bf16[64,1024]{1,0:T(8,128)(2,1)S(1)}, bf16[64,1024]{1,0:T(8,128)(2,1)S(1)}, u32[]{:S(2)}, u32[]{:S(2)}) collective-permute-start(bf16[64,1024]{1,0:T(8,128)(2,1)S(1)} %collective-permute-done.1.refs_2_), channel_id=1, source_target_pairs={{0,1},{1,0},{2,3},{3,2},{4,5},{5,4},{6,7},{7,6},{8,9},{9,8},{10,11... | collective-permute-start | bytes 393224 | tf_op jit(solution)/shard_map/ppermute | solution.py:205
